TPU v7x, 32 devices: a whole 2x2x4 slice. The times are simulated.
32 devices in a mesh: slide: 4 (over x, core), rows: 8 (over z, y).
Axes of the slice: x: 2, y: 2, z: 4, core: 2. Of those that a mesh axis runs over, the one named last changes fastest.
Arguments:
- features: bfloat16 [4, 192, 256, 128], P('slide', None, 'rows'), may hold values from -6 to 6
- depth_kernel: float32 [192, 49], replicated, may hold values from -0.875 to 0.875
- depth_bias: float32 [192], replicated, may hold values from -4 to 4
- norm_gain: float32 [192], replicated, may hold values from 0.1 to 1.9
- norm_bias: float32 [192], replicated, may hold values from -3 to 3
- up_weight: bfloat16 [192, 768], replicated, may hold values from -0.4375 to 0.4375
- up_bias: float32 [768], replicated, may hold values from -3 to 3
- down_weight: bfloat16 [768, 192], replicated, may hold values from -0.21875 to 0.21875
- down_bias: float32 [192], replicated, may hold values from -4 to 4
- layer_scale: float32 [192], replicated, may hold values from 0.2 to 1
- tissue: int32 [4, 8, 4], P('slide', 'rows'), may hold values 0 or 1
- aggregator_order: int32 [4, 32], P('slide'), may hold values from 0 to 31, each once within a row
- tile_cotangent: bfloat16 [4, 32, 192], P('slide', 'rows'), may hold values from -6 to 6
Outputs:
- embedding: float32 [4, 32, 192], P('slide', 'rows')
- input_grad: bfloat16 [4, 192, 256, 128], P('slide', None, 'rows')
- grad_up: float32 [192, 768], replicated
- grad_down: float32 [768, 192], replicated
- grad_kernel: float32 [192, 49], replicated
Inputs may be any that keep to these rules, and one draw needn't show every extreme that they name: `aggregator_order`: each slide's row is a permutation of the 32 positions.
All inputs are finite; a program needn't handle non-finite values. No bound on the sum of `tissue` on one device may be relied on, other than what follows from the above.
Results may differ from a plain program's by a relative error of at most 0.0064.
Values may be sent and summed in bfloat16 or wider, within the bound.
A program may use at most 128 MiB of HBM per device.

v0:
```python
import math
import jax
import jax.numpy as jnp
from jax import lax
from jax.sharding import PartitionSpec as P

TILE = 32


def extended_2(cells, sides, width):
    for axis, dim in sides:
        count = lax.axis_size(axis)
        ends = count - 1
        head = lax.slice_in_dim(cells, 0, width, axis=dim)
        tail = lax.slice_in_dim(cells, cells.shape[dim] - width, cells.shape[dim], axis=dim)
        cells = jnp.concatenate(
            [
                lax.ppermute(tail, axis, [(i, (i + 1) % count) for i in range(ends)]),
                cells,
                lax.ppermute(head, axis, [((i + 1) % count, i) for i in range(ends)]),
            ],
            axis=dim,
        )
    return cells


def depthwise(source, kernel, height, across, mirrored):
    channels = source.shape[0]
    total = jnp.zeros((channels, height, across), jnp.float32)
    for position in range(49):
        row_start = position // 7
        col_start = position % 7
        if mirrored:
            row_start = 6 - row_start
            col_start = 6 - col_start
        window = lax.slice(
            source, (0, row_start, col_start), (channels, row_start + height, col_start + across)
        )
        total = total + kernel[:, position][:, None, None] * window.astype(jnp.float32)
    return total


def gelu_exact(values):
    return 0.5 * values * (1.0 + jax.scipy.special.erf(values * 0.7071067811865476))


def gelu_slope(values):
    cumulative = 0.5 * (1.0 + jax.scipy.special.erf(values * 0.7071067811865476))
    density = jnp.exp(-0.5 * values * values) * 0.3989422804014327
    return cumulative + values * density


def contract_first(left, right):
    return lax.dot_general(
        left, right, (((0,), (0,)), ((), ())), preferred_element_type=jnp.float32
    )


def contract_last(left, right):
    return lax.dot_general(
        left, right, (((1,), (1,)), ((), ())), preferred_element_type=jnp.float32
    )


def block_pass(
    conv_flat,
    image_flat,
    pixel_mask,
    pixel_cotangent,
    norm_gain,
    norm_bias,
    up_weight,
    up_bias,
    down_weight,
    down_bias,
    layer_scale,
):
    average = jnp.mean(conv_flat, axis=0, keepdims=True)
    centered = conv_flat - average
    variance = jnp.mean(centered * centered, axis=0, keepdims=True)
    reciprocal = lax.rsqrt(variance + 1e-06)
    standard = centered * reciprocal
    normed = (standard * norm_gain[:, None] + norm_bias[:, None]).astype(jnp.bfloat16)
    activation_in = contract_first(up_weight, normed) + up_bias[:, None]
    hidden = gelu_exact(activation_in).astype(jnp.bfloat16)
    branch = contract_first(down_weight, hidden) + down_bias[:, None]
    scaled_mask = pixel_mask[None, :] * layer_scale[:, None]
    output = image_flat.astype(jnp.float32) + scaled_mask * branch
    grad_branch = (scaled_mask * pixel_cotangent).astype(jnp.bfloat16)
    grad_hidden = jnp.dot(down_weight, grad_branch, preferred_element_type=jnp.float32)
    grad_activation = (grad_hidden * gelu_slope(activation_in)).astype(jnp.bfloat16)
    grad_normed = jnp.dot(up_weight, grad_activation, preferred_element_type=jnp.float32)
    grad_standard = grad_normed * norm_gain[:, None]
    grad_conv = reciprocal * (
        grad_standard
        - jnp.mean(grad_standard, axis=0, keepdims=True)
        - standard * jnp.mean(grad_standard * standard, axis=0, keepdims=True)
    )
    grad_conv = grad_conv.astype(jnp.bfloat16)
    up_term = contract_last(normed, grad_activation)
    down_term = contract_last(grad_branch, hidden)
    return (output, grad_conv, up_term, down_term)


def on_device(
    features,
    depth_kernel,
    depth_bias,
    norm_gain,
    norm_bias,
    up_weight,
    up_bias,
    down_weight,
    down_bias,
    layer_scale,
    tissue,
    aggregator_order,
    tile_cotangent,
):
    pixels_in = features[0]
    channels, height, across = pixels_in.shape
    tile_size = TILE
    tiles_here = across // tile_size
    hidden_units = up_weight.shape[1]
    extended = extended_2(pixels_in, (("rows", 1),), 3)
    extended = jnp.pad(extended, ((0, 0), (0, 0), (3, 3)))
    convolved = depthwise(extended, depth_kernel, height, across, False) + depth_bias[:, None, None]
    tile_masks = tissue[0, 0].astype(jnp.float32)
    pixel_mask = jnp.broadcast_to(
        tile_masks[None, :, None], (height, tiles_here, tile_size)
    ).reshape(height * across)
    gathered = lax.all_gather(tile_cotangent, "rows", axis=1, tiled=True)[0]
    positions = lax.dynamic_slice_in_dim(
        aggregator_order[0], lax.axis_index("rows") * tiles_here, tiles_here
    )
    wanted = jnp.take(gathered, positions, axis=0).astype(jnp.float32)
    pixel_cotangent = jnp.broadcast_to(
        wanted.T[:, None, :, None], (channels, height, tiles_here, tile_size)
    ).reshape(channels, height * across)
    output, grad_conv, up_term, down_term = block_pass(
        convolved.reshape(channels, height * across),
        pixels_in.reshape(channels, height * across),
        pixel_mask,
        pixel_cotangent,
        norm_gain,
        norm_bias,
        up_weight,
        up_bias,
        down_weight,
        down_bias,
        layer_scale,
    )
    embedding = jnp.mean(output.reshape(channels, height, tiles_here, tile_size), axis=(1, 3)).T[
        None
    ]
    grad_image = grad_conv.reshape(channels, height, across)
    grad_extended = extended_2(grad_image, (("rows", 1),), 3)
    grad_extended = jnp.pad(grad_extended, ((0, 0), (0, 0), (3, 3)))
    backward_conv = depthwise(grad_extended, depth_kernel, height, across, True)
    input_grad = (pixel_cotangent.reshape(channels, height, across) + backward_conv).astype(
        jnp.bfloat16
    )[None]
    kernel_cols = []
    for position in range(49):
        row_start = position // 7
        col_start = position % 7
        window = lax.slice(
            extended, (0, row_start, col_start), (channels, row_start + height, col_start + across)
        )
        kernel_cols.append(
            jnp.einsum("chw,chw->c", grad_image, window, preferred_element_type=jnp.float32)
        )
    kernel_term = jnp.stack(kernel_cols, axis=1)
    loss_norm = 1.0 / math.sqrt(lax.axis_size("slide") * lax.axis_size("rows") * height * across)
    combined = (
        jnp.concatenate(
            [up_term, down_term, kernel_term, jnp.zeros((channels, 15), jnp.float32)], axis=1
        )
        * loss_norm
    )
    totals = lax.psum(combined, ("slide", "rows"))
    grad_up = totals[:, :hidden_units]
    grad_down = totals[:, hidden_units : 2 * hidden_units].T
    grad_kernel = totals[:, 2 * hidden_units : 2 * hidden_units + 49]
    return (embedding, input_grad, grad_up, grad_down, grad_kernel)


def solution(mesh):
    return jax.shard_map(
        on_device,
        mesh=mesh,
        in_specs=(
            P("slide", None, "rows", None),
            P(),
            P(),
            P(),
            P(),
            P(),
            P(),
            P(),
            P(),
            P(),
            P("slide", "rows", None),
            P("slide", None),
            P("slide", "rows", None),
        ),
        out_specs=(P("slide", "rows", None), P("slide", None, "rows", None), P(), P(), P()),
        check_vma=False,
    )
```

profile of v0, /device:TPU:0, one launch (start us, length us, event | category | flops | bytes accessed | tf_op | source)
XLA Modules:
  0.0 483.2 jit_solution(3109074101789072919)
XLA Ops:
  8.6 4.9 %collective-permute-start = (bf16[192,3,128]{2,1,0:T(4,128)(2,1)S(1)}, bf16[192,3,128]{2,1,0:T(4,128)(2,1)S(1)}, u32[]{:S(2)}, u32[]{:S(2)}) collective-permute-start(bf16[192,3,128]{2,1,0:T(4,128)(2,1)S(1)} %get-tuple-element.81), channel_id=1, source_target_pairs={{0,1},{1,2},{2,3},{3,4},{4,5},{5,6},{6,7},{8,9},{9,10},{10,11},{11... | collective-permute-start | bytes 442376 | tf_op jit(solution)/shard_map/ppermute | solution.py:18
  16.0 1.6 fusion.164
  20.0 32.9 %all_gather.3 = bf16[1,32,192]{2,0,1:T(2,128)(2,1)S(1)} all-gather(bf16[1,4,192]{2,0,1:T(2,128)(2,1)S(1)} %copy.129), channel_id=1, replica_groups=mesh['slide'=4,'rows'=8] {'rows'}, dimensions={1}, use_global_device_ids=true | all-gather | bytes 13824 | tf_op jit(solution)/shard_map/all_gather | solution.py:132
  53.6 2.4 broadcast_in_dim.55
  56.0 5.4 %copy.131 = f32[192,4096]{1,0:T(8,128)} copy(f32[192,4096]{0,1:T(8,128)} %bitcast.261) | data formatting | bytes 6291456 | tf_op jit(solution)/shard_map/reshape | solution.py:139
  61.8 2.1 convert.150
  63.9 1.5 fusion.165
  65.5 4.7 select_maximum_fusion.2
  70.6 95.8 %fusion.159 = (f32[32,128]{1,0:T(8,128)S(1)}, f32[192,32,128]{2,1,0:T(8,128)}) fusion(f32[192]{0:T(256)S(1)} %copy-done.71, bf16[192,38,134]{2,1,0:T(8,128)(2,1)} %select_maximum_fusion.2, f32[192]{0:T(256)} %bitcast.50, f32[192]{0:T(256)} %bitcast.49, f32[192]{0:T(256)S(1)} %bitcast.266, bf16[192,3,128]{2,1,0:T(4,128)(2,1)S(1)} %collective-permute-done.1, ...), kind=kLoop, calls=%fused_computation.307 | loop fusion | flops 130543616 | bytes 71128576 | tf_op jit(solution)/shard_map/reduce_sum | solution.py:78
  166.5 2.4 multiply_reduce_fusion
  169.3 7.6 %fusion.7 = (bf16[768,4096]{0,1:T(8,128)(2,1)}, f32[4096,768]{1,0:T(8,128)S(1)}) fusion(f32[768]{0:T(1024)S(1)} %copy-done.72, bf16[192,768]{1,0:T(8,128)(2,1)S(1)} %copy-done, f32[24,8,32,128]{3,2,1,0:T(8,128)S(1)} %bitcast.252, f32[192]{0:T(256)S(1)} %copy-done.73, f32[192]{0:T(256)S(1)} %copy-done.69, f32[4096]{0:T(1024)S(1)} %rsqrt_bitcast_fusion, ...), kind=kOutput, calls=%fused_computation.61 | convolution fusion | flops 1230766080 | bytes 22352384 | tf_op jit(solution)/shard_map/dot_general | solution.py:54
  176.9 7.0 %fusion.5 = bf16[768,4096]{0,1:T(8,128)(2,1)S(1)} fusion(f32[4096,768]{1,0:T(8,128)S(1)} %get-tuple-element.137, bf16[768,192]{0,1:T(8,128)(2,1)S(1)} %copy-done.15, f32[768]{0:T(1024)S(1)} %copy-done.72, f32[192,4096]{1,0:T(8,128)S(1)} %copy-done.6, f32[192]{0:T(256)S(1)} %copy-done.67, f32[4096]{0:T(1024)S(1)} %mul.896), kind=kOutput, calls=%fused_computation.57 | convolution fusion | flops 1244921856 | bytes 22335232 | tf_op jit(solution)/shard_map/dot_general | solution.py:90
  183.9 3.8 fusion.157
  187.7 5.1 %fusion.142 = (f32[4096]{0:T(1024)S(1)}, f32[4096,192]{0,1:T(8,128)}) fusion(f32[24,8,32,128]{3,2,1,0:T(8,128)S(1)} %bitcast.254, f32[4096]{0:T(1024)S(1)} %rsqrt_bitcast_fusion, f32[4096]{0:T(1024)S(1)} %get-tuple-element.134, f32[192]{0:T(256)S(1)} %copy-done.69, bf16[768,4096]{0,1:T(8,128)(2,1)S(1)} %fusion.5, bf16[192,768]{1,0:T(8,128)(2,1)S(1)} %copy-done), kind=kOutput, calls=%fused_computation.257 | convolution fusion | flops 1211887616 | bytes 12927744 | tf_op jit(solution)/shard_map/dot_general | solution.py:92
  192.9 2.0 reduce_sum.48
  194.9 6.1 %fusion.150 = bf16[24,8,32,128]{3,1,2,0:T(8,128)(2,1)S(1)} fusion(f32[24,8,32,128]{3,2,1,0:T(8,128)} %bitcast.251, f32[4096,192]{0,1:T(8,128)} %get-tuple-element.139, f32[4096]{0:T(1024)S(1)} %get-tuple-element.140, f32[4096]{0:T(1024)S(1)} %get-tuple-element.141, f32[4096]{0:T(1024)S(1)} %rsqrt_bitcast_fusion, f32[4096]{0:T(1024)S(1)} %get-tuple-element.134), kind=kLoop, calls=%fused_computation.280 | loop fusion | flops 5505024 | bytes 7929856
  201.4 22.0 %fusion.116 = (f32[192]{0:T(256)}, f32[192]{0:T(256)}, f32[192]{0:T(256)}, f32[192]{0:T(256)}, f32[192]{0:T(256)}, /*index=5*/f32[192]{0:T(256)}, f32[192]{0:T(2...) fusion(bf16[192,38,134]{2,1,0:T(8,128)(2,1)S(1)} %copy-done.2, ...), kind=kLoop, calls=%fused_computation.228 | loop fusion | flops 43250304 | bytes 29898240 | tf_op jit(solution)/shard_map/chw,chw->c/dot_general | solution.py:171
  223.4 22.2 %fusion.137 = (f32[192]{0:T(256)}, f32[192]{0:T(256)}, f32[192]{0:T(256)}, f32[192]{0:T(256)}, f32[192]{0:T(256)}, /*index=5*/f32[192]{0:T(256)}, f32[192]{0:T(2...) fusion(bf16[192,38,134]{2,1,0:T(8,128)(2,1)S(1)} %copy-done.2, ...), kind=kLoop, calls=%fused_computation.249 | loop fusion | flops 43250304 | bytes 29898240 | tf_op jit(solution)/shard_map/chw,chw->c/dot_general | solution.py:171
  245.6 6.3 %fusion.95 = (f32[192]{0:T(256)}, f32[192]{0:T(256)}, f32[192]{0:T(256)}, f32[192]{0:T(256)}, f32[192]{0:T(256)}, /*index=5*/f32[192]{0:T(256)}) fusion(bf16[192,38,134]{2,1,0:T(8,128)(2,1)S(1)} %copy-done.2, bf16[24,8,32,128]{3,2,1,0:T(8,128)(2,1)S(1)} %copy.430), kind=kLoop, calls=%fused_computation.207 | loop fusion | flops 14941056 | bytes 11014656 | tf_op jit(solution)/shard_map/chw,chw->c/dot_general | solution.py:171
  257.0 1.4 copy.144
  258.4 1.4 copy.145
  261.3 1.4 copy.147
  268.3 1.4 copy.153
  269.7 1.4 copy.154
  275.3 1.4 copy.159
  280.9 1.4 copy.164
  285.1 1.4 copy.167
  286.6 1.4 copy.168
  293.7 1.4 copy.174
  295.1 1.4 copy.175
  296.5 1.4 copy.176
  298.0 1.4 copy.178
  299.4 1.4 copy.179
  303.7 1.4 copy.133
  309.3 1.4 copy.138
  310.7 7.6 %fusion.134 = (f32[192]{0:T(256)}, f32[192]{0:T(256)}, f32[192]{0:T(256)}, f32[192]{0:T(256)}, f32[192]{0:T(256)}, /*index=5*/f32[192]{0:T(256)}, f32[192]{0:T(256)}) fusion(bf16[192,3,128]{2,1,0:T(4,128)(2,1)} %copy-done.9, bf16[192,32,128]{2,1,0:T(8,128)(2,1)S(1)} %bitcast.259, bf16[24,8,32,128]{3,2,1,0:T(8,128)(2,1)S(1)} %copy.430, ...), kind=kLoop, calls=%fused_computation.246 | loop fusion | flops 31455936 | bytes 5018880 | tf_op jit(solution)/shard_map/chw,chw->c/dot_general | solution.py:171
  319.8 1.4 copy.142
  326.8 1.4 copy.177
  328.3 6.1 %fusion.154 = f32[192,768]{1,0:T(8,128)} fusion(bf16[768,4096]{0,1:T(8,128)(2,1)} %get-tuple-element.136, f32[192,4096]{1,0:T(8,128)} %copy.131, f32[192]{0:T(256)} %param.22, f32[4096]{0:T(1024)S(1)} %mul.896), kind=kOutput, calls=%fused_computation.304 | convolution fusion | flops 1210318848 | bytes 10044160 | tf_op jit(solution)/shard_map/dot_general | solution.py:60
  335.0 4.0 concatenate.35
  342.4 4.8 collective-permute-start.2
  347.2 9.0 %fusion.13 = f32[192,4096]{1,0:T(8,128)} fusion(bf16[768,4096]{0,1:T(8,128)(2,1)} %get-tuple-element.136, bf16[768,192]{0,1:T(8,128)(2,1)} %param.20, f32[24,8,32,128]{3,2,1,0:T(8,128)} %convert.150, f32[192]{0:T(256)S(1)} %copy-done.70, f32[192]{0:T(256)S(1)} %copy-done.68, f32[4096]{0:T(1024)S(1)} %mul.896), kind=kOutput, calls=%fused_computation.71 | convolution fusion | flops 1211105280 | bytes 12895744 | tf_op jit(solution)/shard_map/dot_general | solution.py:54
  356.1 5.1 %copy.128 = f32[192,4096]{0,1:T(8,128)} copy(f32[192,4096]{1,0:T(8,128)} %fusion.13) | data formatting | bytes 6291456 | tf_op jit(solution)/shard_map/add | solution.py:88
  361.3 2.6 reduce_sum.47
  365.1 3.4 select_maximum_fusion
  368.6 46.0 %fusion.151 = bf16[1,192,32,128]{3,2,1,0:T(8,128)(2,1)} fusion(bf16[192,38,134]{2,1,0:T(8,128)(2,1)S(1)} %select_maximum_fusion, f32[192]{0:T(256)} %bitcast.50, f32[192]{0:T(256)} %bitcast.49, f32[192]{0:T(256)S(1)} %bitcast.267, bf16[192,32,128]{2,1,0:T(8,128)(2,1)S(1)} %bitcast.250, bf16[192,3,128]{2,1,0:T(4,128)(2,1)S(1)} %collective-permute-done.2, ...), kind=kLoop, calls=%fused_computation.284 | loop fusion | flops 123469824 | bytes 74208000 | tf_op jit(solution)/shard_map/broadcast_in_dim | solution.py:160
  414.7 57.5 %all-reduce.4.cloned.1.call-done = f32[192,1600]{1,0:T(8,128)} async-done(((f32[192,1600]{1,0:T(8,128)}), f32[192,1600]{1,0:T(8,128)}) %all-reduce.4.cloned.1.call-update) | async-done | bytes 1228816 | tf_op jit(solution)/shard_map/psum | solution.py:181
  473.8 2.3 slice_bitcast_fusion
  (215 shorter events, 57.3 us)
Async XLA Ops:
  7.2 161.8 %copy-start = (bf16[192,768]{1,0:T(8,128)(2,1)S(1)}, bf16[192,768]{1,0:T(8,128)(2,1)}, u32[]{:S(2)}) copy-start(bf16[192,768]{1,0:T(8,128)(2,1)} %param.18) | copy-start | bytes 884740
  7.2 465.0 %all-reduce.4.cloned.1.call-start = ((), (), s32[]{:S(2)}) async-start(), calls=%async_computation | async-start | bytes 2555904 | tf_op jit(solution)/shard_map/psum | solution.py:181
  8.6 56.9 %collective-permute-start = (bf16[192,3,128]{2,1,0:T(4,128)(2,1)S(1)}, bf16[192,3,128]{2,1,0:T(4,128)(2,1)S(1)}, u32[]{:S(2)}, u32[]{:S(2)}) collective-permute-start(bf16[192,3,128]{2,1,0:T(4,128)(2,1)S(1)} %get-tuple-element.81), channel_id=1, source_target_pairs={{0,1},{1,2},{2,3},{3,4},{4,5},{5,6},{6,7},{8,9},{9,10},{10,11},{11... | collective-permute-start | bytes 442376 | tf_op jit(solution)/shard_map/ppermute | solution.py:18
  13.5 52.0 %collective-permute-start.1 = (bf16[192,3,128]{2,1,0:T(4,128)(2,1)S(1)}, bf16[192,3,128]{2,1,0:T(4,128)(2,1)S(1)}, u32[]{:S(2)}, u32[]{:S(2)}) collective-permute-start(bf16[192,3,128]{2,1,0:T(4,128)(2,1)S(1)} %get-tuple-element.82), channel_id=1, source_target_pairs={{1,0},{2,1},{3,2},{4,3},{5,4},{6,5},{7,6},{9,8},{10,9},{11,10},{12... | collective-permute-start | bytes 442376 | tf_op jit(solution)/shard_map/ppermute | solution.py:20
  15.9 54.4 %copy-start.16 = (f32[192,1]{0,1:T(1,128)}, f32[192,1]{0,1:T(1,128)S(1)}, u32[]{:S(2)}) copy-start(f32[192,1]{0,1:T(1,128)S(1)} %get-tuple-element.85) | copy-start | bytes 2308
  15.9 54.4 %copy-start.18 = (f32[192,1]{0,1:T(1,128)}, f32[192,1]{0,1:T(1,128)S(1)}, u32[]{:S(2)}) copy-start(f32[192,1]{0,1:T(1,128)S(1)} %get-tuple-element.86) | copy-start | bytes 2308
  15.9 54.4 %copy-start.20 = (f32[192,1]{0,1:T(1,128)}, f32[192,1]{0,1:T(1,128)S(1)}, u32[]{:S(2)}) copy-start(f32[192,1]{0,1:T(1,128)S(1)} %get-tuple-element.87) | copy-start | bytes 2308
  15.9 54.4 %copy-start.22 = (f32[192,1]{0,1:T(1,128)}, f32[192,1]{0,1:T(1,128)S(1)}, u32[]{:S(2)}) copy-start(f32[192,1]{0,1:T(1,128)S(1)} %get-tuple-element.88) | copy-start | bytes 2308
  15.9 54.4 %copy-start.24 = (f32[192,1]{0,1:T(1,128)}, f32[192,1]{0,1:T(1,128)S(1)}, u32[]{:S(2)}) copy-start(f32[192,1]{0,1:T(1,128)S(1)} %get-tuple-element.89) | copy-start | bytes 2308
  15.9 54.4 %copy-start.26 = (f32[192,1]{0,1:T(1,128)}, f32[192,1]{0,1:T(1,128)S(1)}, u32[]{:S(2)}) copy-start(f32[192,1]{0,1:T(1,128)S(1)} %get-tuple-element.90) | copy-start | bytes 2308
  15.9 54.4 %copy-start.28 = (f32[192,1]{0,1:T(1,128)}, f32[192,1]{0,1:T(1,128)S(1)}, u32[]{:S(2)}) copy-start(f32[192,1]{0,1:T(1,128)S(1)} %get-tuple-element.91) | copy-start | bytes 2308
  15.9 54.4 %copy-start.30 = (f32[192,1]{0,1:T(1,128)}, f32[192,1]{0,1:T(1,128)S(1)}, u32[]{:S(2)}) copy-start(f32[192,1]{0,1:T(1,128)S(1)} %get-tuple-element.92) | copy-start | bytes 2308
  15.9 54.4 %copy-start.32 = (f32[192,1]{0,1:T(1,128)}, f32[192,1]{0,1:T(1,128)S(1)}, u32[]{:S(2)}) copy-start(f32[192,1]{0,1:T(1,128)S(1)} %get-tuple-element.93) | copy-start | bytes 2308
  15.9 54.4 %copy-start.34 = (f32[192,1]{0,1:T(1,128)}, f32[192,1]{0,1:T(1,128)S(1)}, u32[]{:S(2)}) copy-start(f32[192,1]{0,1:T(1,128)S(1)} %get-tuple-element.94) | copy-start | bytes 2308
  16.0 54.4 %copy-start.36 = (f32[192,1]{0,1:T(1,128)}, f32[192,1]{0,1:T(1,128)S(1)}, u32[]{:S(2)}) copy-start(f32[192,1]{0,1:T(1,128)S(1)} %get-tuple-element.95) | copy-start | bytes 2308
  16.0 54.4 %copy-start.38 = (f32[192,1]{0,1:T(1,128)}, f32[192,1]{0,1:T(1,128)S(1)}, u32[]{:S(2)}) copy-start(f32[192,1]{0,1:T(1,128)S(1)} %get-tuple-element.96) | copy-start | bytes 2308
  16.0 54.4 %copy-start.40 = (f32[192,1]{0,1:T(1,128)}, f32[192,1]{0,1:T(1,128)S(1)}, u32[]{:S(2)}) copy-start(f32[192,1]{0,1:T(1,128)S(1)} %get-tuple-element.97) | copy-start | bytes 2308
  16.0 54.4 %copy-start.42 = (f32[192,1]{0,1:T(1,128)}, f32[192,1]{0,1:T(1,128)S(1)}, u32[]{:S(2)}) copy-start(f32[192,1]{0,1:T(1,128)S(1)} %get-tuple-element.98) | copy-start | bytes 2308
  16.0 54.4 %copy-start.44 = (f32[192,1]{0,1:T(1,128)}, f32[192,1]{0,1:T(1,128)S(1)}, u32[]{:S(2)}) copy-start(f32[192,1]{0,1:T(1,128)S(1)} %get-tuple-element.99) | copy-start | bytes 2308
  16.0 54.4 %copy-start.45 = (f32[192,1]{0,1:T(1,128)}, f32[192,1]{0,1:T(1,128)S(1)}, u32[]{:S(2)}) copy-start(f32[192,1]{0,1:T(1,128)S(1)} %get-tuple-element.100) | copy-start | bytes 2308
  16.0 54.4 %copy-start.46 = (f32[192,1]{0,1:T(1,128)}, f32[192,1]{0,1:T(1,128)S(1)}, u32[]{:S(2)}) copy-start(f32[192,1]{0,1:T(1,128)S(1)} %get-tuple-element.101) | copy-start | bytes 2308
  16.0 54.4 %copy-start.47 = (f32[192,1]{0,1:T(1,128)}, f32[192,1]{0,1:T(1,128)S(1)}, u32[]{:S(2)}) copy-start(f32[192,1]{0,1:T(1,128)S(1)} %get-tuple-element.102) | copy-start | bytes 2308
  16.0 54.4 %copy-start.48 = (f32[192,1]{0,1:T(1,128)}, f32[192,1]{0,1:T(1,128)S(1)}, u32[]{:S(2)}) copy-start(f32[192,1]{0,1:T(1,128)S(1)} %get-tuple-element.103) | copy-start | bytes 2308
  17.6 52.8 %copy-start.49 = (f32[192,1]{0,1:T(1,128)}, f32[192,1]{0,1:T(1,128)S(1)}, u32[]{:S(2)}) copy-start(f32[192,1]{0,1:T(1,128)S(1)} %get-tuple-element.104) | copy-start | bytes 2308
  17.7 52.8 %copy-start.50 = (f32[192,1]{0,1:T(1,128)}, f32[192,1]{0,1:T(1,128)S(1)}, u32[]{:S(2)}) copy-start(f32[192,1]{0,1:T(1,128)S(1)} %get-tuple-element.105) | copy-start | bytes 2308
  17.7 52.8 %copy-start.51 = (f32[192,1]{0,1:T(1,128)}, f32[192,1]{0,1:T(1,128)S(1)}, u32[]{:S(2)}) copy-start(f32[192,1]{0,1:T(1,128)S(1)} %get-tuple-element.106) | copy-start | bytes 2308
  17.7 52.8 %copy-start.52 = (f32[192,1]{0,1:T(1,128)}, f32[192,1]{0,1:T(1,128)S(1)}, u32[]{:S(2)}) copy-start(f32[192,1]{0,1:T(1,128)S(1)} %get-tuple-element.107) | copy-start | bytes 2308
  17.7 52.8 %copy-start.53 = (f32[192,1]{0,1:T(1,128)}, f32[192,1]{0,1:T(1,128)S(1)}, u32[]{:S(2)}) copy-start(f32[192,1]{0,1:T(1,128)S(1)} %get-tuple-element.108) | copy-start | bytes 2308
  17.7 52.8 %copy-start.54 = (f32[192,1]{0,1:T(1,128)}, f32[192,1]{0,1:T(1,128)S(1)}, u32[]{:S(2)}) copy-start(f32[192,1]{0,1:T(1,128)S(1)} %get-tuple-element.109) | copy-start | bytes 2308
  17.7 52.8 %copy-start.55 = (f32[192,1]{0,1:T(1,128)}, f32[192,1]{0,1:T(1,128)S(1)}, u32[]{:S(2)}) copy-start(f32[192,1]{0,1:T(1,128)S(1)} %get-tuple-element.110) | copy-start | bytes 2308
  17.7 52.8 %copy-start.56 = (f32[192,1]{0,1:T(1,128)}, f32[192,1]{0,1:T(1,128)S(1)}, u32[]{:S(2)}) copy-start(f32[192,1]{0,1:T(1,128)S(1)} %get-tuple-element.111) | copy-start | bytes 2308
  17.7 52.8 %copy-start.57 = (f32[192,1]{0,1:T(1,128)}, f32[192,1]{0,1:T(1,128)S(1)}, u32[]{:S(2)}) copy-start(f32[192,1]{0,1:T(1,128)S(1)} %get-tuple-element.112) | copy-start | bytes 2308
  17.7 52.8 %copy-start.58 = (f32[192,1]{0,1:T(1,128)}, f32[192,1]{0,1:T(1,128)S(1)}, u32[]{:S(2)}) copy-start(f32[192,1]{0,1:T(1,128)S(1)} %get-tuple-element.113) | copy-start | bytes 2308
  17.7 52.8 %copy-start.59 = (f32[192,1]{0,1:T(1,128)}, f32[192,1]{0,1:T(1,128)S(1)}, u32[]{:S(2)}) copy-start(f32[192,1]{0,1:T(1,128)S(1)} %get-tuple-element.114) | copy-start | bytes 2308
  17.7 52.8 %copy-start.60 = (f32[192,1]{0,1:T(1,128)}, f32[192,1]{0,1:T(1,128)S(1)}, u32[]{:S(2)}) copy-start(f32[192,1]{0,1:T(1,128)S(1)} %get-tuple-element.115) | copy-start | bytes 2308
  17.8 52.8 %copy-start.61 = (f32[192,1]{0,1:T(1,128)}, f32[192,1]{0,1:T(1,128)S(1)}, u32[]{:S(2)}) copy-start(f32[192,1]{0,1:T(1,128)S(1)} %get-tuple-element.116) | copy-start | bytes 2308
  17.8 52.8 %copy-start.62 = (f32[192,1]{0,1:T(1,128)}, f32[192,1]{0,1:T(1,128)S(1)}, u32[]{:S(2)}) copy-start(f32[192,1]{0,1:T(1,128)S(1)} %get-tuple-element.117) | copy-start | bytes 2308
  17.8 52.8 %copy-start.63 = (f32[192,1]{0,1:T(1,128)}, f32[192,1]{0,1:T(1,128)S(1)}, u32[]{:S(2)}) copy-start(f32[192,1]{0,1:T(1,128)S(1)} %get-tuple-element.118) | copy-start | bytes 2308
  17.8 52.8 %copy-start.64 = (f32[192,1]{0,1:T(1,128)}, f32[192,1]{0,1:T(1,128)S(1)}, u32[]{:S(2)}) copy-start(f32[192,1]{0,1:T(1,128)S(1)} %get-tuple-element.119) | copy-start | bytes 2308
  17.8 52.8 %copy-start.65 = (f32[192,1]{0,1:T(1,128)}, f32[192,1]{0,1:T(1,128)S(1)}, u32[]{:S(2)}) copy-start(f32[192,1]{0,1:T(1,128)S(1)} %get-tuple-element.120) | copy-start | bytes 2308
  17.8 52.8 %copy-start.66 = (f32[192,1]{0,1:T(1,128)}, f32[192,1]{0,1:T(1,128)S(1)}, u32[]{:S(2)}) copy-start(f32[192,1]{0,1:T(1,128)S(1)} %get-tuple-element.121) | copy-start | bytes 2308
  65.5 101.0 %copy-start.7 = (bf16[192,3,128]{2,1,0:T(4,128)(2,1)}, bf16[192,3,128]{2,1,0:T(4,128)(2,1)S(1)}, u32[]{:S(2)}) copy-start(bf16[192,3,128]{2,1,0:T(4,128)(2,1)S(1)} %collective-permute-done) | copy-start | bytes 442372
  65.5 100.9 %copy-start.9 = (bf16[192,3,128]{2,1,0:T(4,128)(2,1)}, bf16[192,3,128]{2,1,0:T(4,128)(2,1)S(1)}, u32[]{:S(2)}) copy-start(bf16[192,3,128]{2,1,0:T(4,128)(2,1)S(1)} %collective-permute-done.1) | copy-start | bytes 442372
  251.8 58.9 %copy-start.5 = (bf16[1,192,32,128]{3,2,1,0:T(8,128)(2,1)S(1)}, bf16[1,192,32,128]{3,2,1,0:T(8,128)(2,1)}, u32[]{:S(2)}) copy-start(bf16[1,192,32,128]{3,2,1,0:T(8,128)(2,1)} %param.13) | copy-start | bytes 4718596
  251.8 58.9 %copy-start.8 = (bf16[192,3,128]{2,1,0:T(4,128)(2,1)S(1)}, bf16[192,3,128]{2,1,0:T(4,128)(2,1)}, u32[]{:S(2)}) copy-start(bf16[192,3,128]{2,1,0:T(4,128)(2,1)} %copy-done.7) | copy-start | bytes 442372
  341.1 23.8 %collective-permute-start.3 = (bf16[192,3,128]{2,1,0:T(4,128)(2,1)}, bf16[192,3,128]{2,1,0:T(4,128)(2,1)S(1)}, u32[]{:S(2)}, u32[]{:S(2)}) collective-permute-start(bf16[192,3,128]{2,1,0:T(4,128)(2,1)} %get-tuple-element.80), channel_id=1, source_target_pairs={{1,0},{2,1},{3,2},{4,3},{5,4},{6,5},{7,6},{9,8},{10,9},{11,10},{12... | collective-permute-start | bytes 442376 | tf_op jit(solution)/shard_map/ppermute | solution.py:20
  342.4 22.7 %collective-permute-start.2 = (bf16[192,3,128]{2,1,0:T(4,128)(2,1)S(1)}, bf16[192,3,128]{2,1,0:T(4,128)(2,1)S(1)}, u32[]{:S(2)}, u32[]{:S(2)}) collective-permute-start(bf16[192,3,128]{2,1,0:T(4,128)(2,1)S(1)} %get-tuple-element.79), channel_id=1, source_target_pairs={{0,1},{1,2},{2,3},{3,4},{4,5},{5,6},{6,7},{8,9},{9,10},{10,11},{11... | collective-permute-start | bytes 442376 | tf_op jit(solution)/shard_map/ppermute | solution.py:18
  368.6 107.5 %copy-start.1 = (bf16[192,768]{1,0:T(8,128)(2,1)S(1)}, bf16[192,768]{1,0:T(8,128)(2,1)}, u32[]{:S(2)}) copy-start(bf16[192,768]{1,0:T(8,128)(2,1)} %param.18) | copy-start | bytes 884740
  (32 other events, 160.2 us)
Sparse Core Ops, SparseCore 0:
  340.4 131.7 all-reduce.3
where the time goes:
time: 493 us; the launch traced here: 483 us
  other arithmetic  227 us (46%)
  local copies, waits for them, and re-layouts  99.7 us (20%)
  waiting for transfers between devices  57.5 us (12%)
  matrix products  38.6 us (8%)
  blocking collectives  32.9 us (7%)
  between operations  15.4 us (3%)
  starting transfers between devices  12.3 us (2%)
    reduce_sum x1, other arithmetic, block_pass(): average = jnp.mean(conv_flat, axis=0, keepdims=True)  95.8 us
    another operation x49, local copies, waits for them, and re-layouts, on_device(): kernel_term = jnp.stack(kernel_cols, axis=1)  68.8 us
    dot_general x4, other arithmetic, on_device(): jnp.einsum('chw,chw->c', grad_image, window, preferred_element_type=jnp.f...  58.1 us
    psum x1, waiting for transfers between devices, on_device(): totals = lax.psum(combined, ('slide', 'rows'))  57.5 us
    broadcast_in_dim x1, other arithmetic, on_device(): (pixel_cotangent.reshape(channels, height, across) + backward_conv).astyp...  46 us
    all_gather x1, blocking collectives, on_device(): gathered = lax.all_gather(tile_cotangent, 'rows', axis=1, tiled=True)[0]  32.9 us
    dot_general x2, matrix products, contract_first(): lax.dot_general(left, right, (((0,), (0,)), ((), ())), preferred_element_...  16.6 us
    dot_general x2, matrix products, contract_last(): lax.dot_general(left, right, (((1,), (1,)), ((), ())), preferred_element_...  9.89 us
  transfers between devices with their start and end apart: 5, of which 1 were waited for; matrix products, arithmetic and copies ran while one was open for 18% of the time, Pallas kernels for 0%

commit v1 on v0

--- a/solution.py
+++ b/solution.py
@@ -5,6 +5,12 @@
 from jax.sharding import PartitionSpec as P
 
 TILE = 32
+
+
+def gather_and_add(block, name):
+    parts = lax.all_gather(block, name, axis=0, tiled=False)
+    total = parts.sum(axis=0)
+    return total
 
 
 def extended_2(cells, sides, width):
@@ -178,7 +184,7 @@
         )
         * loss_norm
     )
-    totals = lax.psum(combined, ("slide", "rows"))
+    totals = gather_and_add(combined, ("slide", "rows"))
     grad_up = totals[:, :hidden_units]
     grad_down = totals[:, hidden_units : 2 * hidden_units].T
     grad_kernel = totals[:, 2 * hidden_units : 2 * hidden_units + 49]

time: 493 us -> 589 us (1.19)
  waiting for transfers between devices: 57.5 us -> 156 us
  local copies, waits for them, and re-layouts: 99.7 us -> 77.2 us
  other arithmetic: 227 us -> 249 us
    all_gather x0 -> x1, waiting for transfers between devices: none -> 155 us  [gather_and_add(): parts = lax.all_gather(block, name, axis=0, tiled=False)]
    another operation x49 -> x0, local copies, waits for them, and re-layouts: 68.8 us -> none  [on_device(): kernel_term = jnp.stack(kernel_cols, axis=1)]
    psum x1 -> x0, waiting for transfers between devices: 57.5 us -> none  [on_device(): totals = lax.psum(combined, ('slide', 'rows'))]
    concatenate x1 -> x50, local copies, waits for them, and re-layouts: 4 us -> 51.4 us  [on_device(): jnp.concatenate([up_term, down_term, kernel_term, jnp.zeros((channels, 15...]
    reduce_sum x0 -> x1, other arithmetic: none -> 14.9 us  [gather_and_add(): total = parts.sum(axis=0)]
  transfers between devices with their start and end apart: 5 -> 5, of which waited for: 1 -> 3; matrix products, arithmetic and copies ran while one was open for 18% -> 15% of each run, Pallas kernels for 0% -> 0%
where the time goes in v1:
time: 589 us; the launch traced here: 579 us
  other arithmetic  249 us (42%)
  waiting for transfers between devices  156 us (26%)
  local copies, waits for them, and re-layouts  77.2 us (13%)
  matrix products  37.9 us (6%)
  blocking collectives  31.4 us (5%)
  between operations  15.7 us (3%)
  starting transfers between devices  12.7 us (2%)
    all_gather x1, waiting for transfers between devices, gather_and_add(): parts = lax.all_gather(block, name, axis=0, tiled=False)  155 us
    reduce_sum x1, other arithmetic, block_pass(): average = jnp.mean(conv_flat, axis=0, keepdims=True)  100 us
    dot_general x4, other arithmetic, on_device(): jnp.einsum('chw,chw->c', grad_image, window, preferred_element_type=jnp.f...  61.8 us
    concatenate x50, local copies, waits for them, and re-layouts, on_device(): jnp.concatenate([up_term, down_term, kernel_term, jnp.zeros((channels, 15...  51.4 us
    broadcast_in_dim x1, other arithmetic, on_device(): (pixel_cotangent.reshape(channels, height, across) + backward_conv).astyp...  44 us
    all_gather x1, blocking collectives, on_device(): gathered = lax.all_gather(tile_cotangent, 'rows', axis=1, tiled=True)[0]  31.4 us
    dot_general x2, matrix products, contract_first(): lax.dot_general(left, right, (((0,), (0,)), ((), ())), preferred_element_...  16.6 us
    reduce_sum x1, other arithmetic, gather_and_add(): total = parts.sum(axis=0)  14.9 us
  transfers between devices with their start and end apart: 5, of which 3 were waited for; matrix products, arithmetic and copies ran while one was open for 15% of the time, Pallas kernels for 0%

profile of v1, /device:TPU:0, one launch (start us, length us, event | category | flops | bytes accessed | tf_op | source)
XLA Modules:
  0.0 579.4 jit_solution(16289628073499132102)
XLA Ops:
  9.9 5.5 collective-permute-start
  16.7 1.7 fusion.162
  21.4 31.4 %all_gather.7 = bf16[1,32,192]{2,0,1:T(2,128)(2,1)S(1)} all-gather(bf16[1,4,192]{2,0,1:T(2,128)(2,1)S(1)} %copy.131), channel_id=1, replica_groups=mesh['slide'=4,'rows'=8] {'rows'}, dimensions={1}, use_global_device_ids=true | all-gather | bytes 13824 | tf_op jit(solution)/shard_map/all_gather | solution.py:138
  53.5 2.4 broadcast_in_dim.55
  55.9 5.5 copy.133
  61.4 1.6 fusion.163
  63.1 4.7 select_maximum_fusion.2
  67.9 100.0 %fusion.157 = (f32[32,128]{1,0:T(8,128)S(1)}, f32[192,32,128]{2,1,0:T(8,128)S(1)}) fusion(f32[192]{0:T(256)} %param.15, bf16[192,38,134]{2,1,0:T(8,128)(2,1)} %select_maximum_fusion.2, f32[192]{0:T(256)} %bitcast.362, f32[192]{0:T(256)} %bitcast.364, f32[192]{0:T(256)S(1)} %bitcast.270, bf16[192,3,128]{2,1,0:T(4,128)(2,1)} %copy-done.7, ...), kind=kLoop, calls=%fused_computation.307 | loop fusion | flops 130543616 | bytes 71128576 | tf_op jit(solution)/shard_map/reduce_sum | solution.py:84
  168.8 7.6 %fusion.7 = (bf16[768,4096]{0,1:T(8,128)(2,1)}, f32[4096,768]{1,0:T(8,128)S(1)}) fusion(f32[768]{0:T(1024)S(1)} %copy-done.94, bf16[192,768]{1,0:T(8,128)(2,1)S(1)} %copy-done, f32[24,8,32,128]{3,2,1,0:T(8,128)S(1)} %bitcast.255, f32[192]{0:T(256)S(1)} %copy-done.95, f32[192]{0:T(256)S(1)} %copy-done.92, f32[4096]{0:T(1024)S(1)} %rsqrt_bitcast_fusion, ...), kind=kOutput, calls=%fused_computation.61 | convolution fusion | flops 1230766080 | bytes 22352384 | tf_op jit(solution)/shard_map/dot_general | solution.py:60
  176.4 7.0 %fusion.5 = bf16[768,4096]{0,1:T(8,128)(2,1)S(1)} fusion(f32[4096,768]{1,0:T(8,128)S(1)} %get-tuple-element.137, bf16[768,192]{0,1:T(8,128)(2,1)S(1)} %copy-done.12, f32[768]{0:T(1024)S(1)} %copy-done.94, f32[192,4096]{1,0:T(8,128)S(1)} %copy-done.6, f32[192]{0:T(256)S(1)} %copy-done.72, f32[4096]{0:T(1024)S(1)} %mul.903), kind=kOutput, calls=%fused_computation.57 | convolution fusion | flops 1244921856 | bytes 22335232 | tf_op jit(solution)/shard_map/dot_general | solution.py:96
  183.4 5.2 fusion.142
  188.5 3.9 convolution_bitcast_fusion.1
  192.4 2.0 reduce_sum.57
  194.5 6.1 %fusion.150 = bf16[24,8,32,128]{3,1,2,0:T(8,128)(2,1)S(1)} fusion(f32[24,8,32,128]{3,2,1,0:T(8,128)} %bitcast.258, f32[4096,192]{0,1:T(8,128)} %get-tuple-element.139, f32[4096]{0:T(1024)S(1)} %get-tuple-element.140, f32[4096]{0:T(1024)S(1)} %get-tuple-element.141, f32[4096]{0:T(1024)S(1)} %rsqrt_bitcast_fusion, f32[4096]{0:T(1024)S(1)} %get-tuple-element.134), kind=kLoop, calls=%fused_computation.280 | loop fusion | flops 5505024 | bytes 7929856
  201.0 6.3 %fusion.95 = (f32[192]{0:T(256)}, f32[192]{0:T(256)S(1)}, f32[192]{0:T(256)S(1)}, f32[192]{0:T(256)S(1)}, f32[192]{0:T(256)S(1)}, /*index=5*/f32[192]{0:T(256)S(1)}) fusion(bf16[192,38,134]{2,1,0:T(8,128)(2,1)S(1)} %copy-done.2, bf16[24,8,32,128]{3,2,1,0:T(8,128)(2,1)S(1)} %copy.432), kind=kLoop, calls=%fused_computation.207 | loop fusion | flops 14941056 | bytes 11014656 | tf_op jit(solution)/shard_map/chw,chw->c/dot_general | solution.py:177
  207.2 22.2 %fusion.116 = (f32[192]{0:T(256)}, f32[192]{0:T(256)}, f32[192]{0:T(256)}, f32[192]{0:T(256)}, f32[192]{0:T(256)}, /*index=5*/f32[192]{0:T(256)}, f32[192]{0:T(2...) fusion(bf16[192,38,134]{2,1,0:T(8,128)(2,1)S(1)} %copy-done.2, ...), kind=kLoop, calls=%fused_computation.228 | loop fusion | flops 43250304 | bytes 29898240 | tf_op jit(solution)/shard_map/chw,chw->c/dot_general | solution.py:177
  229.4 22.0 %fusion.137 = (f32[192]{0:T(256)S(1)}, f32[192]{0:T(256)S(1)}, f32[192]{0:T(256)S(1)}, f32[192]{0:T(256)S(1)}, f32[192]{0:T(256)}, /*index=5*/f32[192]{0:T(256)}...) fusion(bf16[192,38,134]{2,1,0:T(8,128)(2,1)S(1)} %copy-done.2, ...), kind=kLoop, calls=%fused_computation.249 | loop fusion | flops 43250304 | bytes 29898240 | tf_op jit(solution)/shard_map/chw,chw->c/dot_general | solution.py:177
  251.4 5.2 convolution_bitcast_fusion
  257.2 11.4 %fusion.134 = (f32[192]{0:T(256)}, f32[192]{0:T(256)}, f32[192]{0:T(256)}, f32[192]{0:T(256)}, f32[192]{0:T(256)S(1)}, /*index=5*/f32[192]{0:T(256)}, f32[192]{0:T(256)}) fusion(bf16[192,3,128]{2,1,0:T(4,128)(2,1)S(1)} %copy-done.8, bf16[192,32,128]{2,1,0:T(8,128)(2,1)} %bitcast.261, bf16[24,8,32,128]{3,2,1,0:T(8,128)(2,1)S(1)} %copy.432, ...), kind=kLoop, calls=%fused_computation.246 | loop fusion | flops 31455936 | bytes 5018880 | tf_op jit(solution)/shard_map/chw,chw->c/dot_general | solution.py:177
  269.8 1.4 copy.141
  271.2 1.4 copy.142
  272.6 1.4 copy.143
  274.0 1.4 copy.144
  275.4 1.4 copy.145
  276.8 1.4 copy.146
  279.6 1.4 copy.148
  281.0 1.4 copy.149
  282.4 1.4 copy.150
  283.8 1.4 copy.151
  286.6 1.4 copy.153
  288.1 1.4 copy.154
  289.5 1.4 copy.155
  290.9 1.4 copy.156
  293.1 1.4 copy.158
  299.1 1.4 copy.165
  305.1 1.4 copy.172
  311.1 1.4 copy.179
  315.5 4.9 concatenate.195
  320.3 2.5 broadcast_multiply_fusion
  322.9 3.5 convert.150
  326.5 9.1 %fusion.13 = f32[192,4096]{1,0:T(8,128)} fusion(bf16[768,4096]{0,1:T(8,128)(2,1)} %get-tuple-element.136, bf16[768,192]{0,1:T(8,128)(2,1)S(1)} %copy-done.13, f32[24,8,32,128]{3,2,1,0:T(8,128)} %convert.150, f32[192]{0:T(256)S(1)} %copy-done.93, f32[192]{0:T(256)S(1)} %copy-done.73, f32[4096]{0:T(1024)S(1)} %mul.903), kind=kOutput, calls=%fused_computation.71 | convolution fusion | flops 1211105280 | bytes 12895744 | tf_op jit(solution)/shard_map/dot_general | solution.py:60
  335.6 5.1 copy.130
  340.7 2.6 reduce_sum.56
  344.8 4.6 collective-permute-start.2
  353.1 3.4 select_maximum_fusion
  356.9 44.0 %fusion.151 = bf16[1,192,32,128]{3,2,1,0:T(8,128)(2,1)} fusion(bf16[192,38,134]{2,1,0:T(8,128)(2,1)S(1)} %select_maximum_fusion, f32[192]{0:T(256)} %bitcast.363, f32[192]{0:T(256)} %bitcast.365, f32[192]{0:T(256)S(1)} %bitcast.271, bf16[192,32,128]{2,1,0:T(8,128)(2,1)S(1)} %bitcast.254, bf16[192,3,128]{2,1,0:T(4,128)(2,1)S(1)} %collective-permute-done.2, ...), kind=kLoop, calls=%fused_computation.284 | loop fusion | flops 123469824 | bytes 74208000 | tf_op jit(solution)/shard_map/broadcast_in_dim | solution.py:166
  400.9 154.8 %all-gather.2.cloned.1.call-done = f32[32,192,1600]{2,1,0:T(8,128)} async-done(((f32[1,192,1600]{2,1,0:T(8,128)}), f32[32,192,1600]{2,1,0:T(8,128)}) %all-gather.2.cloned.1.call-update) | async-done | bytes 39321616 | tf_op jit(solution)/shard_map/all_gather | solution.py:11
  555.7 14.9 %reduce_sum.59 = f32[192,1600]{1,0:T(8,128)S(1)} reduce(f32[32,192,1600]{2,1,0:T(8,128)} %all-gather.2.cloned.1.call-done, f32[]{:T(128)} %constant.18.clone.1), dimensions={0}, to_apply=%region_5.6 | reduce | flops 9523200 | bytes 40550404 | tf_op jit(solution)/shard_map/reduce_sum | solution.py:12
  (258 shorter events, 37.3 us)
Async XLA Ops:
  7.2 161.2 %copy-start = (bf16[192,768]{1,0:T(8,128)(2,1)S(1)}, bf16[192,768]{1,0:T(8,128)(2,1)}, u32[]{:S(2)}) copy-start(bf16[192,768]{1,0:T(8,128)(2,1)} %param.18) | copy-start | bytes 884740
  7.2 548.5 %all-gather.2.cloned.1.call-start = ((), (), s32[]{:S(2)}) async-start(), calls=%async_computation | async-start | bytes 42172416 | tf_op jit(solution)/shard_map/all_gather | solution.py:11
  8.6 54.5 %collective-permute-start.1 = (bf16[192,3,128]{2,1,0:T(4,128)(2,1)S(1)}, bf16[192,3,128]{2,1,0:T(4,128)(2,1)S(1)}, u32[]{:S(2)}, u32[]{:S(2)}) collective-permute-start(bf16[192,3,128]{2,1,0:T(4,128)(2,1)S(1)} %get-tuple-element.82), channel_id=1, source_target_pairs={{1,0},{2,1},{3,2},{4,3},{5,4},{6,5},{7,6},{9,8},{10,9},{11,10},{12... | collective-permute-start | bytes 442376 | tf_op jit(solution)/shard_map/ppermute | solution.py:26
  9.9 53.2 %collective-permute-start = (bf16[192,3,128]{2,1,0:T(4,128)(2,1)S(1)}, bf16[192,3,128]{2,1,0:T(4,128)(2,1)S(1)}, u32[]{:S(2)}, u32[]{:S(2)}) collective-permute-start(bf16[192,3,128]{2,1,0:T(4,128)(2,1)S(1)} %get-tuple-element.81), channel_id=1, source_target_pairs={{0,1},{1,2},{2,3},{3,4},{4,5},{5,6},{6,7},{8,9},{9,10},{10,11},{11... | collective-permute-start | bytes 442376 | tf_op jit(solution)/shard_map/ppermute | solution.py:24
  16.6 51.2 %copy-start.14 = (f32[192,1]{0,1:T(1,128)}, f32[192,1]{0,1:T(1,128)S(1)}, u32[]{:S(2)}) copy-start(f32[192,1]{0,1:T(1,128)S(1)} %get-tuple-element.86) | copy-start | bytes 2308
  16.6 51.2 %copy-start.16 = (f32[192,1]{0,1:T(1,128)}, f32[192,1]{0,1:T(1,128)S(1)}, u32[]{:S(2)}) copy-start(f32[192,1]{0,1:T(1,128)S(1)} %get-tuple-element.87) | copy-start | bytes 2308
  16.6 51.2 %copy-start.18 = (f32[192,1]{0,1:T(1,128)}, f32[192,1]{0,1:T(1,128)S(1)}, u32[]{:S(2)}) copy-start(f32[192,1]{0,1:T(1,128)S(1)} %get-tuple-element.88) | copy-start | bytes 2308
  16.6 51.2 %copy-start.20 = (f32[192,1]{0,1:T(1,128)}, f32[192,1]{0,1:T(1,128)S(1)}, u32[]{:S(2)}) copy-start(f32[192,1]{0,1:T(1,128)S(1)} %get-tuple-element.89) | copy-start | bytes 2308
  16.6 51.2 %copy-start.22 = (f32[192,1]{0,1:T(1,128)}, f32[192,1]{0,1:T(1,128)S(1)}, u32[]{:S(2)}) copy-start(f32[192,1]{0,1:T(1,128)S(1)} %get-tuple-element.90) | copy-start | bytes 2308
  16.6 51.2 %copy-start.24 = (f32[192,1]{0,1:T(1,128)}, f32[192,1]{0,1:T(1,128)S(1)}, u32[]{:S(2)}) copy-start(f32[192,1]{0,1:T(1,128)S(1)} %get-tuple-element.91) | copy-start | bytes 2308
  16.6 51.2 %copy-start.26 = (f32[192,1]{0,1:T(1,128)}, f32[192,1]{0,1:T(1,128)S(1)}, u32[]{:S(2)}) copy-start(f32[192,1]{0,1:T(1,128)S(1)} %get-tuple-element.92) | copy-start | bytes 2308
  16.6 51.2 %copy-start.28 = (f32[192,1]{0,1:T(1,128)}, f32[192,1]{0,1:T(1,128)S(1)}, u32[]{:S(2)}) copy-start(f32[192,1]{0,1:T(1,128)S(1)} %get-tuple-element.93) | copy-start | bytes 2308
  16.6 51.2 %copy-start.30 = (f32[192,1]{0,1:T(1,128)}, f32[192,1]{0,1:T(1,128)S(1)}, u32[]{:S(2)}) copy-start(f32[192,1]{0,1:T(1,128)S(1)} %get-tuple-element.94) | copy-start | bytes 2308
  16.7 51.2 %copy-start.32 = (f32[192,1]{0,1:T(1,128)}, f32[192,1]{0,1:T(1,128)S(1)}, u32[]{:S(2)}) copy-start(f32[192,1]{0,1:T(1,128)S(1)} %get-tuple-element.95) | copy-start | bytes 2308
  16.7 51.2 %copy-start.34 = (f32[192,1]{0,1:T(1,128)}, f32[192,1]{0,1:T(1,128)S(1)}, u32[]{:S(2)}) copy-start(f32[192,1]{0,1:T(1,128)S(1)} %get-tuple-element.96) | copy-start | bytes 2308
  16.7 51.2 %copy-start.36 = (f32[192,1]{0,1:T(1,128)}, f32[192,1]{0,1:T(1,128)S(1)}, u32[]{:S(2)}) copy-start(f32[192,1]{0,1:T(1,128)S(1)} %get-tuple-element.97) | copy-start | bytes 2308
  16.7 51.2 %copy-start.38 = (f32[192,1]{0,1:T(1,128)}, f32[192,1]{0,1:T(1,128)S(1)}, u32[]{:S(2)}) copy-start(f32[192,1]{0,1:T(1,128)S(1)} %get-tuple-element.98) | copy-start | bytes 2308
  16.7 51.2 %copy-start.40 = (f32[192,1]{0,1:T(1,128)}, f32[192,1]{0,1:T(1,128)S(1)}, u32[]{:S(2)}) copy-start(f32[192,1]{0,1:T(1,128)S(1)} %get-tuple-element.99) | copy-start | bytes 2308
  16.7 51.2 %copy-start.42 = (f32[192,1]{0,1:T(1,128)}, f32[192,1]{0,1:T(1,128)S(1)}, u32[]{:S(2)}) copy-start(f32[192,1]{0,1:T(1,128)S(1)} %get-tuple-element.100) | copy-start | bytes 2308
  16.7 51.2 %copy-start.44 = (f32[192,1]{0,1:T(1,128)}, f32[192,1]{0,1:T(1,128)S(1)}, u32[]{:S(2)}) copy-start(f32[192,1]{0,1:T(1,128)S(1)} %get-tuple-element.101) | copy-start | bytes 2308
  16.7 51.2 %copy-start.46 = (f32[192,1]{0,1:T(1,128)}, f32[192,1]{0,1:T(1,128)S(1)}, u32[]{:S(2)}) copy-start(f32[192,1]{0,1:T(1,128)S(1)} %get-tuple-element.102) | copy-start | bytes 2308
  16.7 51.2 %copy-start.48 = (f32[192,1]{0,1:T(1,128)}, f32[192,1]{0,1:T(1,128)S(1)}, u32[]{:S(2)}) copy-start(f32[192,1]{0,1:T(1,128)S(1)} %get-tuple-element.103) | copy-start | bytes 2308
  167.9 20.6 %copy-start.3 = (f32[192,32,128]{2,1,0:T(8,128)}, f32[192,32,128]{2,1,0:T(8,128)S(1)}, u32[]{:S(2)}) copy-start(f32[192,32,128]{2,1,0:T(8,128)S(1)} %get-tuple-element.78) | copy-start | bytes 9437188
  168.8 7.6 %copy-start.6 = (f32[192,4096]{1,0:T(8,128)S(1)}, f32[192,4096]{1,0:T(8,128)}, u32[]{:S(2)}) copy-start(f32[192,4096]{1,0:T(8,128)} %copy.133) | copy-start | bytes 9437188
  168.8 7.6 %copy-start.12 = (bf16[768,192]{0,1:T(8,128)(2,1)S(1)}, bf16[768,192]{0,1:T(8,128)(2,1)}, u32[]{:S(2)}) copy-start(bf16[768,192]{0,1:T(8,128)(2,1)} %param.20) | copy-start | bytes 884740
  168.8 7.6 %copy-start.72 = (f32[192]{0:T(256)S(1)}, f32[192]{0:T(256)}, u32[]{:S(2)}) copy-start(f32[192]{0:T(256)} %param.22) | copy-start | bytes 2308
  257.0 35.3 %copy-start.91 = (f32[192]{0:T(256)S(1)}, f32[192]{0:T(256)}, u32[]{:S(2)}) copy-start(f32[192]{0:T(256)} %get-tuple-element.46) | copy-start | bytes 2308
  257.0 37.5 %copy-start.90 = (f32[192]{0:T(256)S(1)}, f32[192]{0:T(256)}, u32[]{:S(2)}) copy-start(f32[192]{0:T(256)} %get-tuple-element.45) | copy-start | bytes 2308
  257.0 38.2 %copy-start.89 = (f32[192]{0:T(256)S(1)}, f32[192]{0:T(256)}, u32[]{:S(2)}) copy-start(f32[192]{0:T(256)} %get-tuple-element.44) | copy-start | bytes 2308
  257.0 39.0 %copy-start.88 = (f32[192]{0:T(256)S(1)}, f32[192]{0:T(256)}, u32[]{:S(2)}) copy-start(f32[192]{0:T(256)} %get-tuple-element.43) | copy-start | bytes 2308
  257.1 39.7 %copy-start.87 = (f32[192]{0:T(256)S(1)}, f32[192]{0:T(256)}, u32[]{:S(2)}) copy-start(f32[192]{0:T(256)} %get-tuple-element.42) | copy-start | bytes 2308
  257.1 40.5 %copy-start.86 = (f32[192]{0:T(256)S(1)}, f32[192]{0:T(256)}, u32[]{:S(2)}) copy-start(f32[192]{0:T(256)} %get-tuple-element.41) | copy-start | bytes 2308
  257.1 41.3 %copy-start.85 = (f32[192]{0:T(256)S(1)}, f32[192]{0:T(256)}, u32[]{:S(2)}) copy-start(f32[192]{0:T(256)} %get-tuple-element.40) | copy-start | bytes 2308
  257.1 43.5 %copy-start.84 = (f32[192]{0:T(256)S(1)}, f32[192]{0:T(256)}, u32[]{:S(2)}) copy-start(f32[192]{0:T(256)} %get-tuple-element.39) | copy-start | bytes 2308
  257.1 44.2 %copy-start.83 = (f32[192]{0:T(256)S(1)}, f32[192]{0:T(256)}, u32[]{:S(2)}) copy-start(f32[192]{0:T(256)} %get-tuple-element.38) | copy-start | bytes 2308
  257.1 45.0 %copy-start.82 = (f32[192]{0:T(256)S(1)}, f32[192]{0:T(256)}, u32[]{:S(2)}) copy-start(f32[192]{0:T(256)} %get-tuple-element.37) | copy-start | bytes 2308
  257.1 45.7 %copy-start.81 = (f32[192]{0:T(256)S(1)}, f32[192]{0:T(256)}, u32[]{:S(2)}) copy-start(f32[192]{0:T(256)} %get-tuple-element.36) | copy-start | bytes 2308
  257.1 46.5 %copy-start.80 = (f32[192]{0:T(256)S(1)}, f32[192]{0:T(256)}, u32[]{:S(2)}) copy-start(f32[192]{0:T(256)} %get-tuple-element.35) | copy-start | bytes 2308
  257.1 47.2 %copy-start.79 = (f32[192]{0:T(256)S(1)}, f32[192]{0:T(256)}, u32[]{:S(2)}) copy-start(f32[192]{0:T(256)} %get-tuple-element.34) | copy-start | bytes 2308
  257.1 49.4 %copy-start.78 = (f32[192]{0:T(256)S(1)}, f32[192]{0:T(256)}, u32[]{:S(2)}) copy-start(f32[192]{0:T(256)} %get-tuple-element.33) | copy-start | bytes 2308
  268.6 38.7 %copy-start.77 = (f32[192]{0:T(256)S(1)}, f32[192]{0:T(256)}, u32[]{:S(2)}) copy-start(f32[192]{0:T(256)} %get-tuple-element.32) | copy-start | bytes 2308
  268.6 39.5 %copy-start.76 = (f32[192]{0:T(256)S(1)}, f32[192]{0:T(256)}, u32[]{:S(2)}) copy-start(f32[192]{0:T(256)} %get-tuple-element.31) | copy-start | bytes 2308
  268.6 40.3 %copy-start.75 = (f32[192]{0:T(256)S(1)}, f32[192]{0:T(256)}, u32[]{:S(2)}) copy-start(f32[192]{0:T(256)} %get-tuple-element.30) | copy-start | bytes 2308
  268.6 41.0 %copy-start.74 = (f32[192]{0:T(256)S(1)}, f32[192]{0:T(256)}, u32[]{:S(2)}) copy-start(f32[192]{0:T(256)} %get-tuple-element.29) | copy-start | bytes 2308
  268.6 46.9 %copy-start.11 = (f32[1,192,768]{2,1,0:T(8,128)S(1)}, f32[1,192,768]{2,1,0:T(8,128)}, u32[]{:S(2)}) copy-start(f32[1,192,768]{2,1,0:T(8,128)} %convolution_bitcast_fusion.1) | copy-start | bytes 1769476
  343.5 7.6 %collective-permute-start.3 = (bf16[192,3,128]{2,1,0:T(4,128)(2,1)S(1)}, bf16[192,3,128]{2,1,0:T(4,128)(2,1)S(1)}, u32[]{:S(2)}, u32[]{:S(2)}) collective-permute-start(bf16[192,3,128]{2,1,0:T(4,128)(2,1)S(1)} %get-tuple-element.80), channel_id=1, source_target_pairs={{1,0},{2,1},{3,2},{4,3},{5,4},{6,5},{7,6},{9,8},{10,9},{11,10},{12... | collective-permute-start | bytes 442376 | tf_op jit(solution)/shard_map/ppermute | solution.py:26
  344.8 8.3 %collective-permute-start.2 = (bf16[192,3,128]{2,1,0:T(4,128)(2,1)S(1)}, bf16[192,3,128]{2,1,0:T(4,128)(2,1)S(1)}, u32[]{:S(2)}, u32[]{:S(2)}) collective-permute-start(bf16[192,3,128]{2,1,0:T(4,128)(2,1)S(1)} %get-tuple-element.79), channel_id=1, source_target_pairs={{0,1},{1,2},{2,3},{3,4},{4,5},{5,6},{6,7},{8,9},{9,10},{10,11},{11... | collective-permute-start | bytes 442376 | tf_op jit(solution)/shard_map/ppermute | solution.py:24
  555.7 16.7 %copy-start.1 = (bf16[192,768]{1,0:T(8,128)(2,1)S(1)}, bf16[192,768]{1,0:T(8,128)(2,1)}, u32[]{:S(2)}) copy-start(bf16[192,768]{1,0:T(8,128)(2,1)} %param.18) | copy-start | bytes 884740
  (53 other events, 298.3 us)
Sparse Core Ops, SparseCore 0:
  323.0 232.5 all-gather.1
